TPU v7x, 128 devices: a whole 4x4x4 slice. The times are simulated.
128 devices in a mesh: dp: 4 (over y_hi, core), mp: 32 (over x, z, y_lo).
Axes of the slice: x: 4, y: 4 (y_hi: 2, y_lo: 2; y = y_hi * 2 + y_lo), z: 4, core: 2. Of those that a mesh axis runs over, the one named last changes fastest.
Arguments:
- step_ids: int32 [32, 4], P('dp'), may hold values from 0 to 31999
- prompt_lens: int32 [32], P('dp'), may hold values from 128 to 1024
- embed_table: bfloat16 [32000, 4096], P(None, 'mp'), may hold values from -170 to 170
- attn_gain: bfloat16 [4096], replicated, may hold values from 0.099609375 to 1.8984375
- w_qkv: bfloat16 [3, 4096, 4096], P(None, None, 'mp'), may hold values from -0.09375 to 0.09375
- w_out: bfloat16 [4096, 4096], P('mp'), may hold values from -0.1875 to 0.1875
- key_cache: bfloat16 [32, 32, 1024, 128], P('dp', 'mp'), may hold values from -194 to 194
- value_cache: bfloat16 [32, 32, 1024, 128], P('dp', 'mp'), may hold values from -6 to 6
- reward_pieces: bfloat16 [32, 4096, 4096], P('dp', None, 'mp'), may hold values from -170 to 170
- piece_lens: int32 [32], P('dp'), may hold values from 256 to 4096
- reward_gain: bfloat16 [4096], replicated, may hold values from 0.099609375 to 1.8984375
- w_value: bfloat16 [4096, 2048], P('mp'), may hold values from -0.09375 to 0.09375
- b_value: float32 [2048], replicated, may hold values from -4 to 4
- w_score: float32 [2048], replicated, may hold values from -0.125 to 0.125
- b_score: float32 [1], replicated, may hold values from -3 to 3
Outputs:
- attn_out: bfloat16 [32, 4, 4096], P('dp')
- piece_values: float32 [32, 4096], P('dp', 'mp')
All inputs are finite; a program needn't handle non-finite values.
Results may differ from a plain program's by a relative error of at most 0.015.
Values may be sent and summed in bfloat16 or wider, within the bound.
No kernel may reach another device: no remote copies, remote signals or barrier semaphores. Data moves between devices by JAX's collectives and lax.ppermute only.
A program may use at most 192 MiB of HBM per device.

v0:
```python
import math
import jax
import jax.numpy as jnp
from jax import lax
from jax.sharding import PartitionSpec as P

epsilon = 1e-05
masked = -1e30


def normalize(rows_in, gain_vec):
    widened = rows_in.astype(jnp.float32)
    inverse_rms = lax.rsqrt(jnp.mean(widened * widened, axis=-1, keepdims=True) + epsilon)
    return (widened * inverse_rms * gain_vec.astype(jnp.float32)).astype(jnp.bfloat16)


def rotate(vectors, positions):
    half_dim = vectors.shape[-1] // 2
    frequency = 10000.0 ** (-2.0 * jnp.arange(half_dim, dtype=jnp.float32) / (2 * half_dim))
    angles = positions.astype(jnp.float32)[:, None, None] * frequency
    cosines = jnp.cos(angles)
    sines = jnp.sin(angles)
    first_half = vectors[..., :half_dim]
    second = vectors[..., half_dim:]
    return jnp.concatenate(
        [first_half * cosines - second * sines, second * cosines + first_half * sines], axis=-1
    )


def project(normed, w_qkv, positions, head_dim):
    projected = jnp.einsum("nd,cde->nce", normed, w_qkv, preferred_element_type=jnp.float32)
    head_count = projected.shape[2] // head_dim
    projected = projected.reshape(projected.shape[0], 3, head_count, head_dim)
    queries = rotate(projected[:, 0], positions).astype(jnp.bfloat16)
    new_key = rotate(projected[:, 1], positions).astype(jnp.bfloat16)
    new_value = projected[:, 2].astype(jnp.bfloat16)
    return (queries, new_key, new_value)


def attend(queries, key_cache, value_cache, live_slots, new_keys, new_values, query_steps):
    inverse_root = 1.0 / math.sqrt(queries.shape[-1])
    cache_scores = (
        jnp.einsum("rhqd,rhld->rhql", queries, key_cache, preferred_element_type=jnp.float32)
        * inverse_root
    )
    cache_scores = jnp.where(live_slots[:, None, None, :], cache_scores, masked)
    new_scores = (
        jnp.einsum("rhqd,rhsd->rhqs", queries, new_keys, preferred_element_type=jnp.float32)
        * inverse_root
    )
    causal = jnp.arange(new_keys.shape[2], dtype=jnp.int32)[None, :] <= query_steps[:, None]
    new_scores = jnp.where(causal[None, None], new_scores, masked)
    row_max = jnp.maximum(
        jnp.max(cache_scores, axis=-1, keepdims=True), jnp.max(new_scores, axis=-1, keepdims=True)
    )
    cache_weights = jnp.exp(cache_scores - row_max)
    new_weights = jnp.exp(new_scores - row_max)
    weight_total = jnp.sum(cache_weights, axis=-1) + jnp.sum(new_weights, axis=-1)
    mixed = jnp.einsum(
        "rhql,rhld->rhqd",
        cache_weights.astype(jnp.bfloat16),
        value_cache,
        preferred_element_type=jnp.float32,
    )
    mixed = mixed + jnp.einsum(
        "rhqs,rhsd->rhqd",
        new_weights.astype(jnp.bfloat16),
        new_values,
        preferred_element_type=jnp.float32,
    )
    return (mixed / weight_total[..., None]).astype(jnp.bfloat16)


def combine_heads(partial_sum):
    return lax.psum(partial_sum, "mp").astype(jnp.bfloat16)


def per_device(
    step_ids,
    prompt_lens,
    embed_table,
    attn_gain,
    w_qkv,
    w_out,
    key_cache,
    value_cache,
    reward_pieces,
    piece_lens,
    reward_gain,
    w_value,
    b_value,
    w_score,
    b_score,
):
    row_count, step_count = step_ids.shape
    head_dim = key_cache.shape[3]
    cache_slots = jnp.arange(key_cache.shape[2], dtype=jnp.int32)
    live_slots = cache_slots[None, :] < prompt_lens[:, None]
    key_list = []
    value_list = []
    results = []
    for step_index in range(step_count):
        local_rows = jnp.take(embed_table, step_ids[:, step_index], axis=0)
        full_rows = lax.all_gather(local_rows, "mp", axis=1, tiled=True)
        normed = normalize(full_rows, attn_gain)
        queries, new_key, new_value = project(normed, w_qkv, prompt_lens + step_index, head_dim)
        key_list.append(new_key[:, :, None, :])
        value_list.append(new_value[:, :, None, :])
        head_out = attend(
            queries[:, :, None, :],
            key_cache,
            value_cache,
            live_slots,
            jnp.concatenate(key_list, axis=2),
            jnp.concatenate(value_list, axis=2),
            jnp.array([step_index], dtype=jnp.int32),
        )
        partial_sum = jnp.dot(
            head_out.reshape(row_count, -1), w_out, preferred_element_type=jnp.float32
        )
        results.append(combine_heads(partial_sum[:, None, :]))
    attn_out = jnp.concatenate(results, axis=1)
    normed_pieces = normalize(
        lax.all_to_all(reward_pieces, "mp", split_axis=1, concat_axis=2, tiled=True), reward_gain
    )
    piece_count, seq_local, model_width = normed_pieces.shape
    token_rows = normed_pieces.reshape(piece_count * seq_local, model_width)
    preact = jnp.dot(
        token_rows,
        lax.all_gather(w_value, "mp", axis=0, tiled=True),
        preferred_element_type=jnp.float32,
    )
    hidden = jax.nn.silu(preact + b_value)
    scored = jnp.dot(hidden, w_score, precision=lax.Precision.HIGHEST) + b_score[0]
    scored = scored.reshape(piece_count, seq_local)
    positions_here = lax.axis_index("mp") * seq_local + jnp.arange(seq_local, dtype=jnp.int32)
    piece_values = jnp.where(positions_here[None, :] < piece_lens[:, None], scored, 0.0)
    return (attn_out, piece_values)


def solution(mesh):
    return jax.shard_map(
        per_device,
        mesh=mesh,
        in_specs=(
            P("dp", None),
            P("dp"),
            P(None, "mp"),
            P(),
            P(None, None, "mp"),
            P("mp", None),
            P("dp", "mp", None, None),
            P("dp", "mp", None, None),
            P("dp", None, "mp"),
            P("dp"),
            P(),
            P("mp", None),
            P(),
            P(),
            P(),
        ),
        out_specs=(P("dp", None, None), P("dp", "mp")),
        check_vma=False,
    )
```

profile of v0, /device:TPU:0, one launch (start us, length us, event | category | flops | bytes accessed | tf_op | source)
XLA Modules:
  0.0 725.0 jit_solution(3366700105728323592)
XLA Ops:
  7.2 0.7 all-gather.2.cloned.1.call-update
  7.9 10.5 %copy.97 = bf16[8,4096,128]{2,0,1:T(8,128)(2,1)} copy(bf16[8,4096,128]{2,1,0:T(8,128)(2,1)} %param.29) | data formatting | bytes 16777216 | tf_op args[8]
  18.5 9.6 %all-to-all-start = ((bf16[8,4096,128]{2,0,1:T(8,128)(2,1)}), bf16[8,4096,128]{2,0,1:T(8,128)(2,1)}, u32[]{:S(2)}, u32[]{:S(2)}) async-start(bf16[8,4096,128]{2,0,1:T(8,128)(2,1)} %copy.97), calls=%async_computation | async-start | bytes 16777216 | tf_op jit(solution)/shard_map/all_to_all | solution.py:124
  28.1 5.0 gather_fusion
  33.1 4.9 gather_fusion.3
  38.0 4.9 gather_fusion.2
  43.0 4.9 gather_fusion.1
  48.0 196.1 %all_gather.15 = bf16[8,4096]{1,0:T(8,128)(2,1)S(1)} all-gather(bf16[8,128]{1,0:T(8,128)(2,1)S(1)} %broadcast_select_fusion.3), channel_id=1, replica_groups=mesh['dp'=4,'mp'=32] {'mp'}, dimensions={1}, use_global_device_ids=true | all-gather | bytes 67584 | tf_op jit(solution)/shard_map/all_gather | solution.py:104
  244.2 76.6 %all_gather.18 = bf16[8,4096]{1,0:T(8,128)(2,1)S(1)} all-gather(bf16[8,128]{1,0:T(8,128)(2,1)S(1)} %broadcast_select_fusion), channel_id=1, replica_groups=mesh['dp'=4,'mp'=32] {'mp'}, dimensions={1}, use_global_device_ids=true | all-gather | bytes 67584 | tf_op jit(solution)/shard_map/all_gather | solution.py:104
  320.9 79.8 %all_gather.17 = bf16[8,4096]{1,0:T(8,128)(2,1)S(1)} all-gather(bf16[8,128]{1,0:T(8,128)(2,1)S(1)} %broadcast_select_fusion.1), channel_id=1, replica_groups=mesh['dp'=4,'mp'=32] {'mp'}, dimensions={1}, use_global_device_ids=true | all-gather | bytes 67584 | tf_op jit(solution)/shard_map/all_gather | solution.py:104
  400.7 77.0 %all_gather.16 = bf16[8,4096]{1,0:T(8,128)(2,1)S(1)} all-gather(bf16[8,128]{1,0:T(8,128)(2,1)S(1)} %broadcast_select_fusion.2), channel_id=1, replica_groups=mesh['dp'=4,'mp'=32] {'mp'}, dimensions={1}, use_global_device_ids=true | all-gather | bytes 67584 | tf_op jit(solution)/shard_map/all_gather | solution.py:104
  481.3 0.6 fusion.29
  482.7 0.6 slice.259
  483.8 0.6 fusion.23
  484.4 0.7 fusion.25
  485.1 0.7 fusion.27
  488.4 0.8 fusion.71
  491.1 1.9 fusion.197
  493.0 1.3 copy.132
  494.3 0.7 add.188
  494.9 0.7 slice_bitcast_fusion.9
  495.6 0.7 slice_bitcast_fusion.8
  496.3 0.7 maximum_bitcast_fusion.1
  497.0 0.8 fusion.85
  498.5 158.8 %all-reduce.2 = (bf16[8,1,4096]{2,0,1:T(8,128)(2,1)S(1)}, bf16[8,1,4096]{2,0,1:T(8,128)(2,1)S(1)}, bf16[8,1,4096]{2,0,1:T(8,128)(2,1)S(1)}, bf16[8,1,4096]{2,0,1:T(8,128)(2,1)S(1)}) all-reduce(f32[8,1,4096]{2,0,1:T(8,128)S(1)} %convolution_bitcast_fusion, ...), channel_id=1, replica_groups=mesh['dp'=4,'mp'=32] {'mp'}, use_global_device_ids=true, to_apply=%region_21.23 | all-reduce | flops 131072 | bytes 786432 | tf_op jit(solution)/shard_map/psum | solution.py:75
  657.3 0.9 copy.100
  658.2 0.7 convert_element_type.246
  659.6 13.9 %copy.98 = f32[8,32,128,128]{3,1,2,0:T(8,128)} copy(bf16[8,32,128,128]{3,0,2,1:T(8,128)(2,1)} %bitcast.258) | data formatting | bytes 25165824 | tf_op jit(solution)/shard_map/convert_element_type | solution.py:12
  673.5 8.5 %multiply_reduce_fusion = f32[8,4096]{0,1:T(8,128)S(1)} fusion(bf16[8,4096,128]{2,0,1:T(8,128)(2,1)} %all-to-all-done), kind=kLoop, calls=%fused_computation.7 | loop fusion | flops 12550144 | bytes 8519680 | tf_op jit(solution)/shard_map/reduce_sum | solution.py:13
  682.3 26.2 %fusion.2 = f32[1024,2048]{1,0:T(8,128)S(1)} fusion(bf16[4096,2048]{1,0:T(8,128)(2,1)} %all-gather.2.cloned.1.call-done, f32[128,8,32,128]{3,2,1,0:T(8,128)} %bitcast.281, f32[4096]{0:T(1024)S(1)} %convert_element_type.246, f32[1024]{0:T(1024)S(1)} %rsqrt_bitcast_fusion), kind=kOutput, calls=%fused_computation.8 | convolution fusion | flops 17192452096 | bytes 41963520 | tf_op jit(solution)/shard_map/dot_general | solution.py:128
  708.6 8.8 %fusion.4 = f32[1,1024]{1,0:T(1,128)S(1)} fusion(f32[2048,1]{0,1:T(1,128)S(1)} %bitcast.306, f32[1024,2048]{1,0:T(8,128)S(1)} %fusion.2, f32[2048]{0:T(1024)S(1)} %copy-done.15), kind=kOutput, calls=%fused_computation.9 | convolution fusion | flops 35651584 | bytes 8409088 | tf_op jit(solution)/shard_map/dot_general | solution.py:134
  717.4 0.7 bitcast_select_fusion
  (118 shorter events, 10.6 us)
Async XLA Ops:
  7.2 470.9 %copy-start = (bf16[3,4096,128]{2,1,0:T(8,128)(2,1)S(1)}, bf16[3,4096,128]{2,1,0:T(8,128)(2,1)}, u32[]{:S(2)}) copy-start(bf16[3,4096,128]{2,1,0:T(8,128)(2,1)} %param.25) | copy-start | bytes 9437188
  7.2 675.1 %all-gather.2.cloned.1.call-start = ((), (), s32[]{:S(2)}) async-start(), calls=%async_computation.1 | async-start | bytes 17301504 | tf_op jit(solution)/shard_map/all_gather | solution.py:130
  18.5 9.6 %copy-start.9 = (bf16[4096]{0:T(1024)(128)(2,1)S(1)}, bf16[4096]{0:T(1024)(128)(2,1)}, u32[]{:S(2)}) copy-start(bf16[4096]{0:T(1024)(128)(2,1)} %param.24) | copy-start | bytes 24580
  18.5 9.6 %copy-start.11 = (s32[8,4]{0,1:T(4,128)S(1)}, s32[8,4]{0,1:T(4,128)}, u32[]{:S(2)}) copy-start(s32[8,4]{0,1:T(4,128)} %param.21) | copy-start | bytes 388
  18.5 459.6 %copy-start.8 = (s32[8]{0:T(128)S(1)}, s32[8]{0:T(128)}, u32[]{:S(2)}) copy-start(s32[8]{0:T(128)} %param.22) | copy-start | bytes 100
  18.5 641.1 %all-to-all-start = ((bf16[8,4096,128]{2,0,1:T(8,128)(2,1)}), bf16[8,4096,128]{2,0,1:T(8,128)(2,1)}, u32[]{:S(2)}, u32[]{:S(2)}) async-start(bf16[8,4096,128]{2,0,1:T(8,128)(2,1)} %copy.97), calls=%async_computation | async-start | bytes 16777216 | tf_op jit(solution)/shard_map/all_to_all | solution.py:124
  479.7 1.6 copy-start.2
  480.3 3.5 copy-start.5
  480.8 2.9 copy-start.6
  483.7 2.2 copy-start.3
  484.4 2.0 copy-start.4
  487.3 1.2 copy-start.7
  487.8 0.5 copy-start.12
  488.3 0.9 copy-start.10
  682.3 26.3 %copy-start.14 = (f32[2048]{0:T(1024)S(1)}, f32[2048]{0:T(1024)}, u32[]{:S(2)}) copy-start(f32[2048]{0:T(1024)} %param.34) | copy-start | bytes 24580
  682.3 26.3 %copy-start.15 = (f32[2048]{0:T(1024)S(1)}, f32[2048]{0:T(1024)}, u32[]{:S(2)}) copy-start(f32[2048]{0:T(1024)} %param.33) | copy-start | bytes 24580
  708.6 8.9 %copy-start.13 = (s32[8]{0:T(128)S(1)}, s32[8]{0:T(128)}, u32[]{:S(2)}) copy-start(s32[8]{0:T(128)} %param.30) | copy-start | bytes 100
  708.6 9.5 %copy-start.1 = (bf16[3,4096,128]{2,1,0:T(8,128)(2,1)S(1)}, bf16[3,4096,128]{2,1,0:T(8,128)(2,1)}, u32[]{:S(2)}) copy-start(bf16[3,4096,128]{2,1,0:T(8,128)(2,1)} %param.25) | copy-start | bytes 9437188
Sparse Core Ops, SparseCore 0:
  9.6 472.2 all-gather.1
where the time goes:
time: 726 us; the launch traced here: 725 us
  blocking collectives  588 us (81%)
  local copies, waits for them, and re-layouts  50.6 us (7%)
  matrix products  44 us (6%)
  other arithmetic  16.8 us (2%)
  between operations  15 us (2%)
  starting transfers between devices  9.59 us (1%)
    all_gather x4, blocking collectives, per_device(): full_rows = lax.all_gather(local_rows, 'mp', axis=1, tiled=True)  429 us
    psum x1, blocking collectives, combine_heads(): return lax.psum(partial_sum, 'mp').astype(jnp.bfloat16)  159 us
    dot_general x1, matrix products, per_device(): jnp.dot(token_rows, lax.all_gather(w_value, 'mp', axis=0, tiled=True), pr...  26.2 us
    gather x4, local copies, waits for them, and re-layouts, per_device(): local_rows = jnp.take(embed_table, step_ids[:, step_index], axis=0)  19.8 us
  transfers between devices with their start and end apart: 2, of which 0 were waited for; matrix products, arithmetic and copies ran while one was open for 10% of the time, Pallas kernels for 0%

commit v1 on v0

--- a/solution.py
+++ b/solution.py
@@ -101,7 +101,9 @@
     results = []
     for step_index in range(step_count):
         local_rows = jnp.take(embed_table, step_ids[:, step_index], axis=0)
-        full_rows = lax.all_gather(local_rows, "mp", axis=1, tiled=True)
+        full_rows = jnp.concatenate(
+            lax.all_to_all(jnp.stack([local_rows] * lax.axis_size("mp")), "mp", 0, 0), axis=1
+        )
         normed = normalize(full_rows, attn_gain)
         queries, new_key, new_value = project(normed, w_qkv, prompt_lens + step_index, head_dim)
         key_list.append(new_key[:, :, None, :])

time: 726 us -> 549 us (0.76)
  blocking collectives: 588 us -> 282 us
  waiting for transfers between devices: 0.69 us -> 99.7 us
  starting transfers between devices: 9.59 us -> 30.5 us
    all_gather x4 -> x0, blocking collectives: 429 us -> none  [per_device(): full_rows = lax.all_gather(local_rows, 'mp', axis=1, tiled=True)]
    psum x1, blocking collectives: 159 us -> 282 us  [combine_heads(): return lax.psum(partial_sum, 'mp').astype(jnp.bfloat16)]
    all_gather x1, waiting for transfers between devices: 0.01 us -> 74.5 us  [per_device(): lax.all_gather(w_value, 'mp', axis=0, tiled=True)]
    all_to_all x0 -> x4, starting transfers between devices: none -> 25.3 us  [per_device(): lax.all_to_all(jnp.stack([local_rows] * lax.axis_size('mp')), 'mp', 0, 0)]
    all_to_all x0 -> x4, waiting for transfers between devices: none -> 24.4 us  [per_device(): lax.all_to_all(jnp.stack([local_rows] * lax.axis_size('mp')), 'mp', 0, 0)]
  transfers between devices with their start and end apart: 2 -> 6, of which waited for: 0 -> 4; matrix products, arithmetic and copies ran while one was open for 10% -> 15% of each run, Pallas kernels for 0% -> 0%
where the time goes in v1:
time: 549 us; the launch traced here: 542 us
  blocking collectives  282 us (51%)
  waiting for transfers between devices  99.7 us (18%)
  local copies, waits for them, and re-layouts  52.2 us (10%)
  matrix products  44.1 us (8%)
  starting transfers between devices  30.5 us (6%)
  other arithmetic  18.8 us (3%)
  between operations  15.1 us (3%)
    psum x1, blocking collectives, combine_heads(): return lax.psum(partial_sum, 'mp').astype(jnp.bfloat16)  282 us
    all_gather x1, waiting for transfers between devices, per_device(): lax.all_gather(w_value, 'mp', axis=0, tiled=True)  74.5 us
    dot_general x1, matrix products, per_device(): jnp.dot(token_rows, lax.all_gather(w_value, 'mp', axis=0, tiled=True), pr...  26.2 us
    all_to_all x4, starting transfers between devices, per_device(): lax.all_to_all(jnp.stack([local_rows] * lax.axis_size('mp')), 'mp', 0, 0)  25.3 us
    all_to_all x4, waiting for transfers between devices, per_device(): lax.all_to_all(jnp.stack([local_rows] * lax.axis_size('mp')), 'mp', 0, 0)  24.4 us
    gather x4, local copies, waits for them, and re-layouts, per_device(): local_rows = jnp.take(embed_table, step_ids[:, step_index], axis=0)  19.9 us
    convert_element_type x1, local copies, waits for them, and re-layouts, normalize(): widened = rows_in.astype(jnp.float32)  14 us
    unnamed x42, local copies, waits for them, and re-layouts  11.4 us
  transfers between devices with their start and end apart: 6, of which 4 were waited for; matrix products, arithmetic and copies ran while one was open for 15% of the time, Pallas kernels for 0%

profile of v1, /device:TPU:0, one launch (start us, length us, event | category | flops | bytes accessed | tf_op | source)
XLA Modules:
  0.0 542.1 jit_solution(7642766988164530375)
XLA Ops:
  7.2 0.7 all-gather.2.cloned.1.call-update
  7.9 0.9 compare_and_fusion.2
  8.9 4.9 gather_fusion
  14.5 9.3 %all-to-all-start = ((bf16[32,8,128]{2,1,0:T(8,128)(2,1)}), bf16[32,8,128]{2,1,0:T(8,128)(2,1)S(1)}, u32[]{:S(2)}, u32[]{:S(2)}) async-start(bf16[32,8,128]{2,1,0:T(8,128)(2,1)} %stack.8), calls=%async_computation | async-start | bytes 131072 | tf_op jit(solution)/shard_map/all_to_all | solution.py:105
  23.8 0.7 convert_element_type.256
  24.5 4.9 gather_fusion.3
  29.5 5.0 gather_fusion.2
  34.5 5.0 gather_fusion.1
  39.6 10.4 %copy.97 = bf16[8,4096,128]{2,0,1:T(8,128)(2,1)} copy(bf16[8,4096,128]{2,1,0:T(8,128)(2,1)} %param.29) | data formatting | bytes 16777216 | tf_op args[8]
  52.7 8.3 %all-to-all-start.3 = ((bf16[32,8,128]{2,1,0:T(8,128)(2,1)}), bf16[32,8,128]{2,1,0:T(8,128)(2,1)S(1)}, u32[]{:S(2)}, u32[]{:S(2)}) async-start(bf16[32,8,128]{2,1,0:T(8,128)(2,1)} %stack.11), calls=%async_computation.3 | async-start | bytes 131072 | tf_op jit(solution)/shard_map/all_to_all | solution.py:105
  61.1 8.1 %all-to-all-done.3 = bf16[32,8,128]{2,1,0:T(8,128)(2,1)S(1)} async-done(((bf16[32,8,128]{2,1,0:T(8,128)(2,1)}), bf16[32,8,128]{2,1,0:T(8,128)(2,1)S(1)}, u32[]{:S(2)}, u32[]{:S(2)}) %all-to-all-start.3) | async-done | bytes 65568 | tf_op jit(solution)/shard_map/all_to_all | solution.py:105
  69.9 3.9 all-to-all-start.2
  74.0 8.1 %all-to-all-done.2 = bf16[32,8,128]{2,1,0:T(8,128)(2,1)S(1)} async-done(((bf16[32,8,128]{2,1,0:T(8,128)(2,1)}), bf16[32,8,128]{2,1,0:T(8,128)(2,1)S(1)}, u32[]{:S(2)}, u32[]{:S(2)}) %all-to-all-start.2) | async-done | bytes 65568 | tf_op jit(solution)/shard_map/all_to_all | solution.py:105
  82.7 3.9 all-to-all-start.1
  86.7 8.2 %all-to-all-done.1 = bf16[32,8,128]{2,1,0:T(8,128)(2,1)S(1)} async-done(((bf16[32,8,128]{2,1,0:T(8,128)(2,1)}), bf16[32,8,128]{2,1,0:T(8,128)(2,1)S(1)}, u32[]{:S(2)}, u32[]{:S(2)}) %all-to-all-start.1) | async-done | bytes 65568 | tf_op jit(solution)/shard_map/all_to_all | solution.py:105
  94.9 5.2 all-to-all-start.4
  109.4 0.7 fusion.75
  112.0 1.9 fusion.201
  113.8 1.3 copy.132
  115.1 0.7 add.188
  115.8 0.7 slice_bitcast_fusion.9
  116.5 0.7 slice_bitcast_fusion.8
  117.2 0.7 maximum_bitcast_fusion.1
  117.8 0.8 fusion.89
  119.3 281.8 %all-reduce.2 = (bf16[8,1,4096]{2,0,1:T(8,128)(2,1)S(1)}, bf16[8,1,4096]{2,0,1:T(8,128)(2,1)S(1)}, bf16[8,1,4096]{2,0,1:T(8,128)(2,1)S(1)}, bf16[8,1,4096]{2,0,1:T(8,128)(2,1)S(1)}) all-reduce(f32[8,1,4096]{2,0,1:T(8,128)S(1)} %convolution_bitcast_fusion, ...), channel_id=1, replica_groups=mesh['dp'=4,'mp'=32] {'mp'}, use_global_device_ids=true, to_apply=%region_21.23 | all-reduce | flops 131072 | bytes 786432 | tf_op jit(solution)/shard_map/psum | solution.py:75
  401.2 0.9 copy.100
  402.1 14.0 %copy.98 = f32[8,32,128,128]{3,1,2,0:T(8,128)} copy(bf16[8,32,128,128]{3,0,2,1:T(8,128)(2,1)} %bitcast.310) | data formatting | bytes 25165824 | tf_op jit(solution)/shard_map/convert_element_type | solution.py:12
  416.1 8.5 %multiply_reduce_fusion = f32[8,4096]{0,1:T(8,128)S(1)} fusion(bf16[8,4096,128]{2,0,1:T(8,128)(2,1)} %all-to-all-done.4), kind=kLoop, calls=%fused_computation.7 | loop fusion | flops 12550144 | bytes 8519680 | tf_op jit(solution)/shard_map/reduce_sum | solution.py:13
  424.9 74.5 %all-gather.2.cloned.1.call-done = bf16[4096,2048]{1,0:T(8,128)(2,1)} async-done(((bf16[128,2048]{1,0:T(8,128)(2,1)}), bf16[4096,2048]{1,0:T(8,128)(2,1)}) %all-gather.2.cloned.1.call-update) | async-done | bytes 16777232 | tf_op jit(solution)/shard_map/all_gather | solution.py:132
  499.4 26.2 %fusion.2 = f32[1024,2048]{1,0:T(8,128)S(1)} fusion(bf16[4096,2048]{1,0:T(8,128)(2,1)} %all-gather.2.cloned.1.call-done, f32[128,8,32,128]{3,2,1,0:T(8,128)} %bitcast.333, f32[4096]{0:T(1024)S(1)} %copy-done.8, f32[1024]{0:T(1024)S(1)} %rsqrt_bitcast_fusion), kind=kOutput, calls=%fused_computation.8 | convolution fusion | flops 17192452096 | bytes 41963520 | tf_op jit(solution)/shard_map/dot_general | solution.py:130
  525.7 8.8 %fusion.4 = f32[1,1024]{1,0:T(1,128)S(1)} fusion(f32[2048,1]{0,1:T(1,128)S(1)} %bitcast.358, f32[1024,2048]{1,0:T(8,128)S(1)} %fusion.2, f32[2048]{0:T(1024)S(1)} %copy-done.19), kind=kOutput, calls=%fused_computation.9 | convolution fusion | flops 35651584 | bytes 8409088 | tf_op jit(solution)/shard_map/dot_general | solution.py:136
  534.6 0.7 bitcast_select_fusion
  (134 shorter events, 16.6 us)
Async XLA Ops:
  7.2 93.1 %copy-start = (bf16[3,4096,128]{2,1,0:T(8,128)(2,1)S(1)}, bf16[3,4096,128]{2,1,0:T(8,128)(2,1)}, u32[]{:S(2)}) copy-start(bf16[3,4096,128]{2,1,0:T(8,128)(2,1)} %param.25) | copy-start | bytes 9437188
  7.2 492.2 %all-gather.2.cloned.1.call-start = ((), (), s32[]{:S(2)}) async-start(), calls=%async_computation.5 | async-start | bytes 17301504 | tf_op jit(solution)/shard_map/all_gather | solution.py:132
  14.5 37.5 %all-to-all-start = ((bf16[32,8,128]{2,1,0:T(8,128)(2,1)}), bf16[32,8,128]{2,1,0:T(8,128)(2,1)S(1)}, u32[]{:S(2)}, u32[]{:S(2)}) async-start(bf16[32,8,128]{2,1,0:T(8,128)(2,1)} %stack.8), calls=%async_computation | async-start | bytes 131072 | tf_op jit(solution)/shard_map/all_to_all | solution.py:105
  39.5 10.4 %copy-start.11 = (bf16[4096]{0:T(1024)(128)(2,1)S(1)}, bf16[4096]{0:T(1024)(128)(2,1)}, u32[]{:S(2)}) copy-start(bf16[4096]{0:T(1024)(128)(2,1)} %param.31) | copy-start | bytes 24580
  39.5 11.7 %copy-start.9 = (s32[8]{0:T(128)S(1)}, s32[8]{0:T(128)}, u32[]{:S(2)}) copy-start(s32[8]{0:T(128)} %param.22) | copy-start | bytes 100
  51.2 58.0 %copy-start.13 = (pred[4]{0:T(512)(128)(4,1)}, pred[4]{0:T(512)(128)(4,1)S(1)}, u32[]{:S(2)}) copy-start(pred[4]{0:T(512)(128)(4,1)S(1)} %iota_compare_fusion.1) | copy-start | bytes 16
  51.2 58.0 %copy-start.14 = (pred[3]{0:T(512)(128)(4,1)}, pred[3]{0:T(512)(128)(4,1)S(1)}, u32[]{:S(2)}) copy-start(pred[3]{0:T(512)(128)(4,1)S(1)} %iota_compare_fusion.2) | copy-start | bytes 13
  52.7 16.6 %all-to-all-start.3 = ((bf16[32,8,128]{2,1,0:T(8,128)(2,1)}), bf16[32,8,128]{2,1,0:T(8,128)(2,1)S(1)}, u32[]{:S(2)}, u32[]{:S(2)}) async-start(bf16[32,8,128]{2,1,0:T(8,128)(2,1)} %stack.11), calls=%async_computation.3 | async-start | bytes 131072 | tf_op jit(solution)/shard_map/all_to_all | solution.py:105
  69.9 12.2 %all-to-all-start.2 = ((bf16[32,8,128]{2,1,0:T(8,128)(2,1)}), bf16[32,8,128]{2,1,0:T(8,128)(2,1)S(1)}, u32[]{:S(2)}, u32[]{:S(2)}) async-start(bf16[32,8,128]{2,1,0:T(8,128)(2,1)} %stack.10), calls=%async_computation.2 | async-start | bytes 131072 | tf_op jit(solution)/shard_map/all_to_all | solution.py:105
  82.7 12.2 %all-to-all-start.1 = ((bf16[32,8,128]{2,1,0:T(8,128)(2,1)}), bf16[32,8,128]{2,1,0:T(8,128)(2,1)S(1)}, u32[]{:S(2)}, u32[]{:S(2)}) async-start(bf16[32,8,128]{2,1,0:T(8,128)(2,1)} %stack.9), calls=%async_computation.1 | async-start | bytes 131072 | tf_op jit(solution)/shard_map/all_to_all | solution.py:105
  94.9 307.2 %all-to-all-start.4 = ((bf16[8,4096,128]{2,0,1:T(8,128)(2,1)}), bf16[8,4096,128]{2,0,1:T(8,128)(2,1)}, u32[]{:S(2)}, u32[]{:S(2)}) async-start(bf16[8,4096,128]{2,0,1:T(8,128)(2,1)} %copy.97), calls=%async_computation.4 | async-start | bytes 16777216 | tf_op jit(solution)/shard_map/all_to_all | solution.py:126
  101.4 2.9 copy-start.2
  102.0 2.3 copy-start.5
  102.5 3.9 copy-start.6
  105.2 2.2 copy-start.3
  105.8 2.0 copy-start.4
  106.5 2.9 copy-start.10
  108.7 0.7 copy-start.7
  109.3 0.8 copy-start.12
  109.4 1.6 copy-start.15
  416.1 83.3 %copy-start.8 = (f32[4096]{0:T(1024)S(1)}, f32[4096]{0:T(1024)}, u32[]{:S(2)}) copy-start(f32[4096]{0:T(1024)} %convert_element_type.298) | copy-start | bytes 49156
  499.4 26.2 %copy-start.18 = (f32[2048]{0:T(1024)S(1)}, f32[2048]{0:T(1024)}, u32[]{:S(2)}) copy-start(f32[2048]{0:T(1024)} %param.34) | copy-start | bytes 24580
  499.4 26.3 %copy-start.19 = (f32[2048]{0:T(1024)S(1)}, f32[2048]{0:T(1024)}, u32[]{:S(2)}) copy-start(f32[2048]{0:T(1024)} %param.33) | copy-start | bytes 24580
  525.7 8.9 %copy-start.16 = (s32[8]{0:T(128)S(1)}, s32[8]{0:T(128)}, u32[]{:S(2)}) copy-start(s32[8]{0:T(128)} %param.30) | copy-start | bytes 100
  525.7 8.9 %copy-start.17 = (s32[128]{0:T(128)S(1)}, s32[128]{0:T(128)}, u32[]{:S(2)}) copy-start(s32[128]{0:T(128)} %iota_add_fusion) | copy-start | bytes 1540
  525.7 9.5 %copy-start.1 = (bf16[3,4096,128]{2,1,0:T(8,128)(2,1)S(1)}, bf16[3,4096,128]{2,1,0:T(8,128)(2,1)}, u32[]{:S(2)}) copy-start(bf16[3,4096,128]{2,1,0:T(8,128)(2,1)} %param.25) | copy-start | bytes 9437188
Sparse Core Ops, SparseCore 0:
  9.6 489.7 all-gather.1
